TPU v7x, 1024 devices: a whole 4x4x32 slice. The times are simulated.
1024 devices in a mesh: dp: 128 (over x_hi, z, core), space: 8 (over x_lo, y).
Axes of the slice: x: 4 (x_hi: 2, x_lo: 2; x = x_hi * 2 + x_lo), y: 4, z: 32, core: 2. Of those that a mesh axis runs over, the one named last changes fastest.
Arguments:
- features: bfloat16 [128, 40, 37, 1024], P('dp', 'space'), may hold values from -6 to 6
- weights: bfloat16 [3, 9, 1024, 128], P(None, None, 'space'), may hold values from -0.0625 to 0.0625
- bias: float32 [3, 128], replicated, may hold values from -3 to 3
- grad_out: bfloat16 [128, 40, 37, 384], P('dp', 'space'), may hold values from -6 to 6
Outputs:
- activations: bfloat16 [128, 40, 37, 384], P('dp', 'space')
- input_grad: bfloat16 [128, 40, 37, 1024], P('dp', 'space')
- weight_grad: float32 [3, 9, 1024, 128], P(None, None, 'space')
- bias_grad: float32 [3, 128], replicated
All inputs are finite; a program needn't handle non-finite values.
Results may differ from a plain program's by a relative error of at most 0.0049.
Values may be sent and summed in bfloat16 or wider, within the bound.
A program may use at most 64 MiB of HBM per device.

v0:
```python
import jax
import jax.numpy as jnp
from jax import lax
from jax.sharding import PartitionSpec as P

dilations = (12, 24, 36)
offsets = tuple(((row_shift, col_shift) for row_shift in (-1, 0, 1) for col_shift in (-1, 0, 1)))
margin = 36


def shifted_windows(padded, spacing, sign, all_rows, columns):
    pieces = []
    for shift_y, shift_x in offsets:
        row_start = margin + sign * shift_y * spacing
        col_start = margin + sign * shift_x * spacing
        pieces.append(
            padded[:, row_start : row_start + all_rows, col_start : col_start + columns, :]
        )
    return jnp.concatenate(pieces, axis=3)


def per_device(features, weights, bias, grad_out):
    images, row_count, columns, _ = features.shape
    outputs = weights.shape[3]
    spread = lax.all_to_all(features, "space", split_axis=3, concat_axis=1, tiled=True)
    all_rows = spread.shape[1]
    channels = spread.shape[3]
    padded_in = jnp.pad(spread, ((0, 0), (margin, margin), (margin, margin), (0, 0)))
    stacked = [shifted_windows(padded_in, spacing, 1, all_rows, columns) for spacing in dilations]

    def branch_partial(branch):
        kernel = weights[branch].reshape(9 * channels, outputs)
        return jnp.einsum(
            "bhwc,co->bhwo", stacked[branch], kernel, preferred_element_type=jnp.float32
        )

    joined = jnp.concatenate([branch_partial(branch) for branch in range(3)], axis=3)
    summed = lax.psum_scatter(joined, "space", scatter_dimension=1, tiled=True)
    pre_act = summed + bias.reshape(-1)
    squash = jax.nn.sigmoid(pre_act)
    active = (pre_act * squash).astype(jnp.bfloat16)
    slope_terms = squash * (1.0 + pre_act * (1.0 - squash))
    grad_local = (grad_out.astype(jnp.float32) * slope_terms).astype(jnp.bfloat16)
    grad_full = lax.all_gather(grad_local, "space", axis=1, tiled=True)
    weight_scale = 1.0 / (images * lax.axis_size("dp"))
    weight_terms = []
    bias_terms = []
    for branch in range(3):
        first_col = branch * outputs
        branch_grad = grad_full[:, :, :, first_col : first_col + outputs]
        weight_part = jnp.einsum(
            "bhwc,bhwo->co", stacked[branch], branch_grad, preferred_element_type=jnp.float32
        ).reshape(9, channels, outputs)
        bias_part = jnp.sum(branch_grad.astype(jnp.float32), axis=(0, 1, 2))
        weight_terms.append(weight_part)
        bias_terms.append(bias_part)
    padded_grad = jnp.pad(grad_full, ((0, 0), (margin, margin), (margin, margin), (0, 0)))
    grad_stack = jnp.concatenate(
        [
            shifted_windows(
                padded_grad[:, :, :, branch * outputs : (branch + 1) * outputs],
                spacing,
                -1,
                all_rows,
                columns,
            )
            for branch, spacing in enumerate(dilations)
        ],
        axis=3,
    )
    kernel_back = jnp.transpose(weights, (0, 1, 3, 2)).reshape(27 * outputs, channels)
    input_sum = jnp.einsum(
        "bhwo,oc->bhwc", grad_stack, kernel_back, preferred_element_type=jnp.float32
    )
    weight_sum = jnp.stack(weight_terms)
    bias_sum = jnp.stack(bias_terms)
    weight_sum, bias_sum = lax.psum((weight_sum, bias_sum), "dp")
    input_grad = lax.all_to_all(
        input_sum.astype(jnp.bfloat16), "space", split_axis=1, concat_axis=3, tiled=True
    )
    return (active, input_grad, weight_sum * weight_scale, bias_sum * weight_scale)


def solution(mesh):
    placed = (
        P("dp", "space", None, None),
        P(None, None, "space", None),
        P(),
        P("dp", "space", None, None),
    )
    return jax.shard_map(
        per_device,
        mesh=mesh,
        in_specs=placed,
        out_specs=(
            P("dp", "space", None, None),
            P("dp", "space", None, None),
            P(None, None, "space", None),
            P(),
        ),
        check_vma=False,
    )
```

profile of v0, /device:TPU:1, one launch (start us, length us, event | category | flops | bytes accessed | tf_op | source)
XLA Modules:
  0.0 1255.4 jit_solution(17304912986206712427)
XLA Ops:
  7.2 2.6 copy.40
  9.8 2.7 reshape.83
  12.5 5.9 all-to-all-start
  18.5 0.9 fusion.97
  19.4 5.5 all-to-all-done
  25.0 2.2 reshape.84
  27.2 1.0 copy.41
  31.4 1.2 fusion.23
  32.6 1.2 fusion.20
  33.8 1.2 fusion.17
  35.2 3.7 copy.46
  39.0 1.3 dynamic-slice
  41.0 120.7 %all-reduce.8.cloned.1.call-done = f32[1,40,37,384]{3,0,2,1:T(1,128)} async-done(((f32[1,40,37,384]{3,0,2,1:T(1,128)}), f32[1,40,37,384]{3,0,2,1:T(1,128)}) %all-reduce.8.cloned.1.call-update) | async-done | bytes 2273296
  161.7 1.9 fusion.96
  164.5 1.1 copy.53
  165.7 1.3 multiply_convert_fusion
  167.6 54.3 %all-gather.2.cloned.1.call-done = bf16[1,40,37,384]{3,2,0,1:T(8,128)(2,1)} async-done(((bf16[1,5,37,384]{3,2,0,1:T(8,128)(2,1)}), bf16[1,40,37,384]{3,2,0,1:T(8,128)(2,1)}) %all-gather.2.cloned.1.call-update) | async-done | bytes 1136656 | tf_op jit(solution)/shard_map/all_gather | solution.py:44
  221.9 1.4 copy.49
  223.4 3.3 fusion.29
  226.7 1.2 fusion.26
  228.6 1.2 fusion.32
  229.8 0.9 fusion.41
  230.7 1.4 pad_maximum_fusion.1
  232.1 0.9 fusion.42
  233.0 0.8 fusion.43
  233.8 0.9 fusion.44
  234.7 0.8 slice_dynamic-update-slice_fusion.2
  236.4 0.9 fusion.46
  237.3 0.9 fusion.47
  238.2 0.9 fusion.48
  240.7 0.9 fusion.51
  241.6 0.8 fusion.52
  242.4 0.9 slice_dynamic-update-slice_fusion.1
  244.1 0.9 fusion.54
  244.9 0.8 fusion.55
  246.6 0.8 fusion.57
  247.4 0.8 fusion.58
  248.3 0.9 fusion.59
  249.1 0.8 fusion.60
  250.0 0.8 slice_dynamic-update-slice_fusion
  251.6 0.8 fusion.62
  252.5 0.8 fusion.63
  254.1 6.9 fusion.38
  261.8 3.5 all-to-all-start.1
  265.5 263.8 %psum.15 = f32[3,128]{1,0:T(4,128)S(1)} all-reduce(f32[3,128]{1,0:T(4,128)S(1)} %pad_maximum_fusion.2), channel_id=1, replica_groups=mesh['dp'=128,'space'=8] {'dp'}, use_global_device_ids=true, to_apply=%region_5.6 | all-reduce | flops 384 | bytes 3072 | tf_op jit(solution)/shard_map/psum | solution.py:77
  530.0 1.0 all_to_all.33
  531.0 715.1 %all-reduce.6.cloned.1.call-done = f32[3,9,128,128]{3,2,1,0:T(8,128)} async-done(((f32[3,9,128,128]{3,2,1,0:T(8,128)}), f32[3,9,128,128]{3,2,1,0:T(8,128)}) %all-reduce.6.cloned.1.call-update) | async-done | bytes 1769488 | tf_op jit(solution)/shard_map/psum | solution.py:77
  1246.0 2.9 broadcast_multiply_fusion
  (69 shorter events, 13.2 us)
Async XLA Ops:
  7.2 11.3 copy-start.5
  12.5 12.5 all-to-all-start
  18.4 143.3 %all-reduce.8.cloned.1.call-start = ((), (), s32[]{:S(2)}) async-start(), calls=%async_computation.4 | async-start | bytes 4546560
  29.4 4.4 copy-start.3
  30.2 1.2 copy-start.8
  30.4 2.2 copy-start.2
  30.9 1.7 copy-start.7
  31.3 2.5 copy-start
  31.4 2.5 copy-start.6
  35.2 126.5 %copy-start.9 = (bf16[1,5,37,384]{3,2,1,0:T(8,128)(2,1)S(1)}, bf16[1,5,37,384]{3,2,1,0:T(8,128)(2,1)}, u32[]{:S(2)}) copy-start(bf16[1,5,37,384]{3,2,1,0:T(8,128)(2,1)} %param.7) | copy-start | bytes 426244
  35.2 126.5 %copy-start.10 = (f32[3,128]{1,0:T(4,128)S(1)}, f32[3,128]{1,0:T(4,128)}, u32[]{:S(2)}) copy-start(f32[3,128]{1,0:T(4,128)} %param.6) | copy-start | bytes 4612
  39.0 182.9 %all-gather.2.cloned.1.call-start = ((), (), s32[]{:S(2)}) async-start(), calls=%async_computation.2 | async-start | bytes 1382400 | tf_op jit(solution)/shard_map/all_gather | solution.py:44
  164.3 1081.8 %all-reduce.6.cloned.1.call-start = ((), (), s32[]{:S(2)}) async-start(), calls=%async_computation.3 | async-start | bytes 3538944 | tf_op jit(solution)/shard_map/psum | solution.py:77
  223.4 3.3 copy-start.4
  226.7 2.0 copy-start.1
  261.8 268.1 %all-to-all-start.1 = ((bf16[1,40,37,128]{3,2,0,1:T(8,128)(2,1)}), bf16[1,40,37,128]{3,2,0,1:T(8,128)(2,1)S(1)}, u32[]{:S(2)}, u32[]{:S(2)}) async-start(bf16[1,40,37,128]{3,2,0,1:T(8,128)(2,1)} %copy.54), calls=%async_computation.1 | async-start | bytes 819200 | tf_op jit(solution)/shard_map/all_to_all | solution.py:78
Sparse Core Ops, SparseCore 0:
  39.1 122.5 all-reduce.7
  165.0 56.9 all-gather.1
  232.2 1013.7 all-reduce.5
where the time goes:
time: 1260 us
  waiting for transfers between devices  896 us (71%)
  blocking collectives  264 us (21%)
  local copies, waits for them, and re-layouts  47 us (4%)
  matrix products  16.1 us (1%)
  between operations  14.8 us (1%)
    psum x1, waiting for transfers between devices, per_device(): weight_sum, bias_sum = lax.psum((weight_sum, bias_sum), 'dp')  715 us
    psum x1, blocking collectives, per_device(): weight_sum, bias_sum = lax.psum((weight_sum, bias_sum), 'dp')  264 us
    unnamed x4, waiting for transfers between devices  121 us
    all_gather x1, waiting for transfers between devices, per_device(): grad_full = lax.all_gather(grad_local, 'space', axis=1, tiled=True)  54.3 us
    unnamed x75, local copies, waits for them, and re-layouts  36 us
  transfers between devices with their start and end apart: 5, of which 4 were waited for; matrix products, arithmetic and copies ran while one was open for 3% of the time, Pallas kernels for 0%

commit v1 on v0

v1 whole, which is shorter than its diff:
```python
import jax
import jax.numpy as jnp
from jax import lax
from jax.experimental import pallas as pl
from jax.experimental.pallas import tpu as pltpu
from jax.sharding import PartitionSpec as P

MESH = pl.DeviceIdType.MESH
BF = jnp.bfloat16
F32 = jnp.float32

Z = 32
ROWS = 20
COLS = 37
PITCH = 48
LEFT = 40
TAPS = 28
PAD = 18


def body(
    feat, w, bias, go, act_o, ig_o, wg_o, bg_o,
    Xr, S, XV, XT, Wf, WT, Pt, RP, GOr, AC, Gr, GVp, WG, IG, IGb,
    SC, RC, SX, RX, T2, SZ1, RZ1, T3, SZ2, RZ2, AA, bsum,
    xs, xr, gos, gor, ws, wr, wl, ps, pr, gs, gr, acs, acr, igs, igr,
    cs, cr, x_s, x_r, z1s, z1r, z2s, z2r, y2s, y2r, y1s, y1r, yxs, yxr, ycs, ycr,
):
    dp = lax.axis_index("dp")
    s = lax.axis_index("space")
    c = lax.rem(dp, 2)
    z = lax.rem(dp // 2, Z)
    u = dp // (2 * Z)
    p = s // 4
    q = lax.rem(s, 4)
    za = lax.rem(z, 4)
    zb = z // 4

    def flip(v, d, n):
        out = v
        bit = 1
        while bit < n:
            if d & bit:
                out = out + bit - 2 * bit * lax.rem(v // bit, 2)
            bit *= 2
        return out

    def dev(uu=None, zz=None, cc=None, pp=None, qq=None):
        uu = u if uu is None else uu
        zz = z if zz is None else zz
        cc = c if cc is None else cc
        pp = p if pp is None else pp
        qq = q if qq is None else qq
        return (uu * (2 * Z) + zz * 2 + cc, pp * 4 + qq)

    peers = [dev(pp=flip(p, d // 4, 2), qq=flip(q, d % 4, 4)) for d in range(1, 8)]
    peers += [dev(cc=1 - c), dev(uu=1 - u), dev(uu=1 - u, pp=1 - p)]
    peers += [dev(zz=zb * 4 + flip(za, d, 4)) for d in range(1, 4)]
    peers += [dev(zz=flip(zb, d, 8) * 4 + za) for d in range(1, 8)]
    barrier = pltpu.get_barrier_semaphore()
    for peer in peers:
        pl.semaphore_signal(barrier, inc=1, device_id=peer, device_id_type=MESH)
    pl.semaphore_wait(barrier, len(peers))

    def remote(src, dst, send, recv, peer):
        return pltpu.make_async_remote_copy(
            src_ref=src, dst_ref=dst, send_sem=send, recv_sem=recv, device_id=peer, device_id_type=MESH
        )

    def arrived(ref, sem):
        pltpu.make_async_copy(ref, ref, sem).wait()

    def feature_copies(i, start):
        row = 5 * s + i
        pp = lax.rem(row, 2)
        n = row // 2
        for qq in range(4):
            away = jnp.logical_or(pp != p, qq != q)
            for h in range(2):
                src = feat.at[0, i, :, pl.ds((qq + 4 * h) * 128, 128)]
                dst = Xr.at[n, :, pl.ds(h * 128, 128)]

                @pl.when(away)
                def _():
                    copy = remote(src, dst, xs.at[i, qq, h], xr.at[n, h], dev(pp=pp, qq=qq))
                    if start:
                        copy.start()
                    else:
                        copy.wait_send()

                if start:
                    @pl.when(jnp.logical_not(away))
                    def _():
                        pltpu.make_async_copy(src, dst, xr.at[n, h]).start()

    lax.fori_loop(0, 5, lambda i, x: (feature_copies(i, True), x)[1], 0)

    def weight_copies():
        own = Wf.at[:, pl.ds(p * 128, 128), :]
        first = remote(
            w.at[pl.ds(0, 14)], Wf.at[pl.ds(0, 14), pl.ds(p * 128, 128), :], ws.at[0], wr.at[0], dev(pp=1 - p)
        )
        second = remote(
            w.at[pl.ds(14, 13)], Wf.at[pl.ds(14, 13), pl.ds(p * 128, 128), :], ws.at[1], wr.at[1],
            dev(uu=1 - u, pp=1 - p),
        )
        return first, second, pltpu.make_async_copy(w, own, wl.at[0])

    for copy in weight_copies():
        copy.start()

    def grad_copies(i, start):
        row = 5 * s + i
        pp = lax.rem(row, 2)
        qq = row // 10
        slot = lax.rem(row // 2, 5)
        away = jnp.logical_or(pp != p, qq != q)

        @pl.when(away)
        def _():
            copy = remote(go.at[0, i], GOr.at[slot], gos.at[i], gor.at[slot], dev(pp=pp, qq=qq))
            if start:
                copy.start()
            else:
                copy.wait_send()

        if start:
            @pl.when(jnp.logical_not(away))
            def _():
                pltpu.make_async_copy(go.at[0, i], GOr.at[slot], gor.at[slot]).start()

    lax.fori_loop(0, 5, lambda i, x: (grad_copies(i, True), x)[1], 0)

    def clear(n, x):
        S[n] = jnp.zeros((128, 384), F32)
        return x

    lax.fori_loop(0, ROWS, clear, 0)

    def clear_pad(n, x):
        for k in range(3):
            GVp[k, n] = jnp.zeros((PITCH, 384), BF)
            GVp[k, PAD + ROWS + n] = jnp.zeros((PITCH, 384), BF)
        return x

    lax.fori_loop(0, PAD, clear_pad, 0)
    for h in range(2):
        WG[27, h] = jnp.zeros((128, 128), F32)

    shifts = (0, -12, 12, -24, 24, -36, 36)

    def spread(n, x):
        for h in range(2):
            arrived(Xr.at[n, :, pl.ds(h * 128, 128)], xr.at[n, h])
        S[n, LEFT : LEFT + COLS, 0:256] = Xr[n].astype(F32)
        for v, d in enumerate(shifts):
            XV[v, n] = S[n, LEFT + d : LEFT + d + PITCH, 0:256].astype(BF)
        return x

    lax.fori_loop(0, ROWS, spread, 0)
    arrived(w, wl.at[0])
    arrived(Wf.at[pl.ds(0, 14), pl.ds((1 - p) * 128, 128), :], wr.at[0])
    arrived(Wf.at[pl.ds(14, 13), pl.ds((1 - p) * 128, 128), :], wr.at[1])

    def partial_copy(k, d):
        qq = flip(q, d, 4)
        return remote(
            Pt.at[k, pl.ds(5 * qq, 5)], RP.at[k, d - 1], ps.at[k, d - 1], pr.at[k, d - 1], dev(qq=qq)
        )

    def gather_copy(k, d):
        rows = Gr.at[k, pl.ds(5 * q, 5)]
        return remote(rows, rows, gs.at[k, d - 1], gr.at[k, d - 1], dev(qq=flip(q, d, 4)))

    for k in range(3):
        for a in (0, -1, 1):
            sh = 6 * (k + 1) * a
            n0, n1 = max(0, -sh), ROWS - max(0, sh)
            rows = n1 - n0
            left = jnp.concatenate(
                [XV[v, n0 + sh : n1 + sh] for v in (1 + 2 * k, 0, 2 + 2 * k)], axis=2
            ).reshape(rows * PITCH, 768)
            t = 9 * k + 3 * (a + 1)
            right = Wf[t : t + 3].reshape(768, 128)
            part = jnp.dot(left, right, preferred_element_type=F32).reshape(rows, PITCH, 128)[:, :40]
            if a == 0:
                Pt[k] = part
            else:
                Pt[k, n0:n1] += part
        for d in range(1, 4):
            partial_copy(k, d).start()

    for j in range(8):
        lo, hi = 128 * j, min(960, 128 * j + 128)
        piece = XV[0].reshape(ROWS * PITCH, 256)[lo:hi].astype(F32)
        if hi - lo < 128:
            piece = jnp.concatenate([piece, jnp.zeros((128 - (hi - lo), 256), F32)], axis=0)
        XT[:, lo : lo + 128] = jnp.transpose(piece).astype(BF)

    def turn(t, x):
        WT[t] = jnp.transpose(Wf[t].astype(F32)).astype(BF)
        return x

    lax.fori_loop(0, 27, turn, 0)
    for i in range(5):
        arrived(GOr.at[i], gor.at[i])

    for k in range(3):
        for d in range(1, 4):
            arrived(RP.at[k, d - 1], pr.at[k, d - 1])
        lanes = slice(128 * k, 128 * (k + 1))
        for i in range(5):
            pre = Pt[k, 5 * q + i] + RP[k, 0, i] + RP[k, 1, i] + RP[k, 2, i] + bias[k : k + 1, :]
            pre = pre[:COLS]
            squash = jax.nn.sigmoid(pre)
            AC[i, :, lanes] = (pre * squash).astype(BF)
            slope = squash * (1.0 + pre * (1.0 - squash))
            Gr[k, 5 * q + i] = (GOr[i, :, lanes].astype(F32) * slope).astype(BF)
        for d in range(1, 4):
            gather_copy(k, d).start()

    def act_copies(i, start):
        row = 10 * q + p + 2 * i
        owner = row // 5
        local = lax.rem(row, 5)
        away = owner != s
        dst = act_o.at[0, local]

        @pl.when(away)
        def _():
            copy = remote(AC.at[i], dst, acs.at[i], acr.at[local], (dp, owner))
            if start:
                copy.start()
            else:
                copy.wait_send()

        if start:
            @pl.when(jnp.logical_not(away))
            def _():
                pltpu.make_async_copy(AC.at[i], dst, acr.at[local]).start()

    lax.fori_loop(0, 5, lambda i, x: (act_copies(i, True), x)[1], 0)

    spans = ((0, 9), (9, 9), (18, 10))

    def core_copy(k):
        lo, size = spans[k]
        return remote(
            SC.at[pl.ds(lo, size)], RC.at[pl.ds(lo, size)], cs.at[k], cr.at[k], dev(cc=1 - c)
        )

    def cross_copy(k, d):
        lo, size = spans[k]
        h, uu = flip(p, d % 2, 2), flip(u, d // 2, 2)
        return remote(
            SX.at[h, uu, pl.ds(lo, size)], RX.at[d - 1, pl.ds(lo, size)], x_s.at[k, d - 1], x_r.at[k, d - 1],
            dev(uu=uu, pp=h),
        )

    def cross_stage(k):
        lo, size = spans[k]
        arrived(RC.at[pl.ds(lo, size)], cr.at[k])

        def add(t, x):
            for h in range(2):
                for uu in range(2):
                    here = WG[t, h, pl.ds(c * 64 + uu * 32, 32), :]
                    SX[h, uu, t] = (here + RC[t, h, uu * 32 : uu * 32 + 32].astype(F32)).astype(BF)
            T2[t] = WG[t, p, pl.ds(c * 64 + u * 32, 32), :] + RC[t, p, pl.ds(u * 32, 32), :].astype(F32)
            return x

        lax.fori_loop(lo, lo + size, add, 0)
        for d in range(1, 4):
            cross_copy(k, d).start()

    for k in range(3):
        for d in range(1, 4):
            arrived(Gr.at[k, pl.ds(5 * flip(q, d, 4), 5)], gr.at[k, d - 1])

        def widen(n, total):
            row = Gr[k, n].astype(F32)
            S[n, LEFT : LEFT + COLS, 256:384] = row
            for cc in range(3):
                d = -12 * (k + 1) * (cc - 1)
                GVp[k, PAD + n, :, 128 * cc : 128 * cc + 128] = S[n, LEFT + d : LEFT + d + PITCH, 256:384].astype(BF)
            return total + jnp.sum(row, axis=0, keepdims=True)

        bsum[k : k + 1, :] = lax.fori_loop(0, ROWS, widen, jnp.zeros((1, 128), F32))
        flat = GVp[k].reshape((ROWS + 2 * PAD) * PITCH, 384)
        for a in (-1, 0, 1):
            sh = 6 * (k + 1) * a
            n0, n1 = max(0, sh), ROWS + min(0, sh)
            f0 = (PITCH * n0) // 128 * 128
            f1 = -(-(PITCH * n1) // 128) * 128
            base = (PAD - sh) * PITCH
            res = jnp.dot(XT[:, f0:f1], flat[base + f0 : base + f1], preferred_element_type=F32)
            for cc in range(3):
                for h in range(2):
                    WG[9 * k + 3 * (a + 1) + cc, h] = res[128 * h : 128 * h + 128, 128 * cc : 128 * cc + 128]
        if k == 2:
            for h in range(2):
                WG[27, h, 0:3] = bsum[0:3]
        lo, size = spans[k]

        def stage(t, x):
            for h in range(2):
                SC[t, h] = WG[t, h, pl.ds((1 - c) * 64, 64), :].astype(BF)
            return x

        lax.fori_loop(lo, lo + size, stage, 0)
        core_copy(k).start()
        if k > 0:
            cross_stage(k - 1)
    cross_stage(2)

    for k in range(3):
        for a in (0, -1, 1):
            sh = 6 * (k + 1) * a
            n0, n1 = max(0, sh), ROWS + min(0, sh)
            rows = n1 - n0
            left = GVp[k, PAD + n0 - sh : PAD + n1 - sh].reshape(rows * PITCH, 384)
            t = 9 * k + 3 * (a + 1)
            right = WT[t : t + 3].reshape(384, 256)
            part = jnp.dot(left, right, preferred_element_type=F32).reshape(rows, PITCH, 256)
            if k == 0 and a == 0:
                IG[...] = part
            else:
                IG[n0:n1] += part

    def input_copies(n, start):
        row = 2 * n + p
        owner = row // 5
        local = lax.rem(row, 5)
        away = owner != s
        for h in range(2):
            src = IGb.at[n, :, pl.ds(h * 128, 128)]
            dst = ig_o.at[0, local, :, pl.ds((q + 4 * h) * 128, 128)]

            @pl.when(away)
            def _():
                copy = remote(src, dst, igs.at[n, h], igr.at[local, q, h], (dp, owner))
                if start:
                    copy.start()
                else:
                    copy.wait_send()

            if start:
                @pl.when(jnp.logical_not(away))
                def _():
                    pltpu.make_async_copy(src, dst, igr.at[local, q, h]).start()

    def finish(n, x):
        IGb[n] = IG[n, :COLS].astype(BF)
        input_copies(n, True)
        return x

    lax.fori_loop(0, ROWS, finish, 0)

    for k in range(3):
        for d in range(1, 4):
            lo, size = spans[k]
            arrived(RX.at[d - 1, pl.ds(lo, size)], x_r.at[k, d - 1])

    def first_copy(d):
        ta = flip(za, d, 4)
        return remote(SZ1.at[ta], RZ1.at[d - 1], z1s.at[d - 1], z1r.at[d - 1], dev(zz=zb * 4 + ta))

    def sum_x(tb, x):
        for ta in range(4):
            t = 4 * tb + ta
            T2[t] = T2[t] + RX[0, t].astype(F32) + RX[1, t].astype(F32) + RX[2, t].astype(F32)
            SZ1[ta, tb] = T2[t].astype(BF)
        return x

    lax.fori_loop(0, 7, sum_x, 0)
    for d in range(1, 4):
        first_copy(d).start()

    for d in range(1, 4):
        arrived(RZ1.at[d - 1], z1r.at[d - 1])

    def sum_z(tb, x):
        T3[tb] = T2[4 * tb + za] + RZ1[0, tb].astype(F32) + RZ1[1, tb].astype(F32) + RZ1[2, tb].astype(F32)
        SZ2[tb] = T3[tb].astype(BF)
        return x

    lax.fori_loop(0, 7, sum_z, 0)

    def second_copy(tb):
        return remote(SZ2.at[tb], RZ2.at[zb], z2s.at[tb], z2r.at[zb], dev(zz=tb * 4 + za))

    def back_copy(b):
        own = AA.at[c, u, za, zb]
        return remote(own, own, y2s.at[b], y2r.at[zb], dev(zz=b * 4 + za))

    for tb in range(7):
        @pl.when(zb != tb)
        def _():
            second_copy(tb).start()

    @pl.when(zb < 7)
    def _():
        total = T3[zb]
        for b in range(8):
            @pl.when(zb != b)
            def _():
                arrived(RZ2.at[b], z2r.at[b])
        for b in range(8):
            total = total + jnp.where(zb != b, RZ2[b].astype(F32), 0.0)
        AA[c, u, za, zb] = (total * (1.0 / 128.0)).astype(BF)
        for b in range(8):
            @pl.when(zb != b)
            def _():
                back_copy(b).start()

    for b in range(7):
        @pl.when(zb != b)
        def _():
            arrived(AA.at[c, u, za, b], y2r.at[b])

    def around_copy(d):
        mine = AA.at[c, u, za]
        return remote(mine, mine, y1s.at[d - 1], y1r.at[d - 1], dev(zz=zb * 4 + flip(za, d, 4)))

    for d in range(1, 4):
        around_copy(d).start()
    for d in range(1, 4):
        arrived(AA.at[c, u, flip(za, d, 4)], y1r.at[d - 1])
    across = remote(AA.at[c, u], AA.at[c, u], yxs.at[0], yxr.at[0], dev(uu=1 - u))
    across.start()
    arrived(AA.at[c, 1 - u], yxr.at[0])
    beside = remote(AA.at[c], AA.at[c], ycs.at[0], ycr.at[0], dev(cc=1 - c))
    beside.start()
    arrived(AA.at[1 - c], ycr.at[0])

    def write(tb, x):
        for ta in range(4):
            t = 4 * tb + ta

            @pl.when(t < 27)
            def _():
                for cc in range(2):
                    for uu in range(2):
                        wg_o[t, cc * 64 + uu * 32 : cc * 64 + uu * 32 + 32, :] = AA[cc, uu, ta, tb].astype(F32)
        return x

    lax.fori_loop(0, 7, write, 0)
    bg_o[...] = AA[0, 0, 3, 6].astype(F32)[0:3]

    lax.fori_loop(0, 5, lambda i, x: (feature_copies(i, False), x)[1], 0)
    lax.fori_loop(0, 5, lambda i, x: (grad_copies(i, False), x)[1], 0)
    lax.fori_loop(0, 5, lambda i, x: (act_copies(i, False), x)[1], 0)
    lax.fori_loop(0, ROWS, lambda n, x: (input_copies(n, False), x)[1], 0)
    first, second, _ = weight_copies()
    first.wait_send()
    second.wait_send()
    for k in range(3):
        for d in range(1, 4):
            partial_copy(k, d).wait_send()
            gather_copy(k, d).wait_send()
            cross_copy(k, d).wait_send()
        core_copy(k).wait_send()
    for d in range(1, 4):
        first_copy(d).wait_send()
        around_copy(d).wait_send()
    for tb in range(7):
        @pl.when(zb != tb)
        def _():
            second_copy(tb).wait_send()

    @pl.when(zb < 7)
    def _():
        for b in range(8):
            @pl.when(zb != b)
            def _():
                back_copy(b).wait_send()

    across.wait_send()
    beside.wait_send()
    for i in range(5):
        arrived(act_o.at[0, i], acr.at[i])
        for qq in range(4):
            for h in range(2):
                arrived(ig_o.at[0, i, :, pl.ds((qq + 4 * h) * 128, 128)], igr.at[i, qq, h])


def per_device(features, weights, bias, grad_out):
    dma = pltpu.SemaphoreType.DMA
    V = pltpu.VMEM
    anywhere = pl.BlockSpec(memory_space=pl.ANY)
    vmem = pl.BlockSpec(memory_space=pltpu.VMEM)
    scratch = [
        V((ROWS, COLS, 256), BF), V((ROWS, 128, 384), F32), V((7, ROWS, PITCH, 256), BF), V((256, 1024), BF),
        V((27, 256, 128), BF), V((27, 128, 256), BF), V((3, ROWS, 40, 128), F32), V((3, 3, 5, 40, 128), F32),
        V((5, COLS, 384), BF), V((5, COLS, 384), BF), V((3, ROWS, COLS, 128), BF),
        V((3, ROWS + 2 * PAD, PITCH, 384), BF), V((TAPS, 2, 128, 128), F32), V((ROWS, PITCH, 256), F32),
        V((ROWS, COLS, 256), BF),
        V((TAPS, 2, 64, 128), BF), V((TAPS, 2, 64, 128), BF), V((2, 2, TAPS, 32, 128), BF), V((3, TAPS, 32, 128), BF),
        V((TAPS, 32, 128), F32), V((4, 7, 32, 128), BF), V((3, 7, 32, 128), BF), V((7, 32, 128), F32),
        V((7, 32, 128), BF), V((8, 32, 128), BF), V((2, 2, 4, 7, 32, 128), BF), V((8, 128), F32),
        dma((5, 4, 2)), dma((ROWS, 2)), dma((5,)), dma((5,)), dma((2,)), dma((2,)), dma((1,)),
        dma((3, 3)), dma((3, 3)), dma((3, 3)), dma((3, 3)), dma((5,)), dma((5,)), dma((ROWS, 2)), dma((5, 4, 2)),
        dma((3,)), dma((3,)), dma((3, 3)), dma((3, 3)), dma((3,)), dma((3,)), dma((7,)), dma((8,)),
        dma((8,)), dma((8,)), dma((3,)), dma((3,)), dma((1,)), dma((1,)), dma((1,)), dma((1,)),
    ]
    act, ig, wg, bg = pl.pallas_call(
        body,
        out_shape=(
            jax.ShapeDtypeStruct((1, 5, COLS, 384), BF),
            jax.ShapeDtypeStruct((1, 5, COLS, 1024), BF),
            jax.ShapeDtypeStruct((27, 128, 128), F32),
            jax.ShapeDtypeStruct((3, 128), F32),
        ),
        in_specs=[anywhere, anywhere, vmem, anywhere],
        out_specs=(anywhere, anywhere, vmem, vmem),
        scratch_shapes=scratch,
        compiler_params=pltpu.CompilerParams(
            collective_id=0, has_side_effects=True, vmem_limit_bytes=56 << 20
        ),
        name="pyramid",
    )(features, weights.reshape(27, 128, 128), bias, grad_out)
    return act, ig, wg.reshape(3, 9, 128, 128), bg


def solution(mesh):
    placed = (
        P("dp", "space", None, None),
        P(None, None, "space", None),
        P(),
        P("dp", "space", None, None),
    )
    return jax.shard_map(
        per_device,
        mesh=mesh,
        in_specs=placed,
        out_specs=(
            P("dp", "space", None, None),
            P("dp", "space", None, None),
            P(None, None, "space", None),
            P(),
        ),
        check_vma=False,
    )
```

time: 1260 us -> 145 us (0.12)
  waiting for transfers between devices: 896 us -> 0 us
  blocking collectives: 264 us -> 0 us
  Pallas kernels: 0 us -> 137 us
  local copies, waits for them, and re-layouts: 47 us -> 6.82 us
  matrix products: 16.1 us -> 0 us
  between operations: 14.8 us -> 0.64 us
    psum x1 -> x0, waiting for transfers between devices: 715 us -> none  [per_device(): weight_sum, bias_sum = lax.psum((weight_sum, bias_sum), 'dp')]
    psum x1 -> x0, blocking collectives: 264 us -> none  [per_device(): weight_sum, bias_sum = lax.psum((weight_sum, bias_sum), 'dp')]
    pallas_call x0 -> x1, Pallas kernels: none -> 137 us  [per_device(): pl.pallas_call(body, out_shape=(jax.ShapeDtypeStruct((1, 5, COLS, 384), B...]
    unnamed x4 -> x0, waiting for transfers between devices: 121 us -> none
    all_gather x1 -> x0, waiting for transfers between devices: 54.3 us -> none  [per_device(): grad_full = lax.all_gather(grad_local, 'space', axis=1, tiled=True)]
    unnamed x75 -> x6, local copies, waits for them, and re-layouts: 36 us -> 6.82 us
    dot_general x7 -> x0, matrix products: 16.1 us -> none  [the longest x1 6.89 us: per_device(): jnp.einsum('bhwo,oc->bhwc', grad_stack, kernel_back, preferred_element_ty...]
  transfers between devices with their start and end apart: 5 -> 0, of which waited for: 4 -> 0; matrix products, arithmetic and copies ran while one was open for 3% -> 0% of each run, Pallas kernels for 0% -> 0%
where the time goes in v1:
time: 145 us
  Pallas kernels  137 us (94%)
  local copies, waits for them, and re-layouts  6.82 us (5%)
    pallas_call x1, Pallas kernels, per_device(): pl.pallas_call(body, out_shape=(jax.ShapeDtypeStruct((1, 5, COLS, 384), B...  137 us
    unnamed x6, local copies, waits for them, and re-layouts  6.82 us

profile of v1, /device:TPU:1, one launch (start us, length us, event | category | flops | bytes accessed | tf_op | source)
XLA Modules:
  0.0 144.8 jit_solution(8473515103653091927)
XLA Ops:
  0.6 137.3 %pyramid.1 = (bf16[1,5,37,384]{3,2,1,0:T(8,128)(2,1)}, bf16[1,5,37,1024]{3,2,1,0:T(8,128)(2,1)}, f32[27,128,128]{2,1,0:T(8,128)}, f32[3,128]{1,0:T(4,128)}) custom-call(bf16[1,5,37,1024]{3,2,1,0:T(8,128)(2,1)} %feat.1, bf16[27,128,128]{2,1,0:T(8,128)(2,1)} %bitcast.3, f32[3,128]{1,0:T(4,128)} %bias.1, bf16[1,5,37,384]{3,2,1,0:T(8,128)(2,1)} %go.1), custom_call_target="tpu_custom_call" | custom-call | tf_op jit(solution)/shard_map/pyramid/pallas_call | solution.py:505
  138.0 1.6 %copy.12 = bf16[1,5,37,384]{3,2,1,0:T(8,128)(2,1)} copy(bf16[1,5,37,384]{3,2,1,0:T(8,128)(2,1)} %get-tuple-element.16) | data formatting | bytes 284160
  139.6 1.8 %copy.13 = bf16[1,5,37,1024]{3,2,1,0:T(8,128)(2,1)} copy(bf16[1,5,37,1024]{3,2,1,0:T(8,128)(2,1)} %get-tuple-element.17) | data formatting | bytes 757760
  141.3 0.0 copy-start
  141.3 2.9 %copy.14 = f32[3,9,128,128]{3,2,1,0:T(8,128)} copy(f32[3,9,128,128]{3,2,1,0:T(8,128)} %bitcast.2) | data formatting | bytes 3538944
  144.2 0.0 copy-done
  144.2 0.6 copy.15
Async XLA Ops:
  141.3 2.9 %copy-start = (f32[3,128]{1,0:T(4,128)S(1)}, f32[3,128]{1,0:T(4,128)}, u32[]{:S(2)}) copy-start(f32[3,128]{1,0:T(4,128)} %get-tuple-element.19) | copy-start | bytes 4612

commit v2 on v1

--- a/solution.py
+++ b/solution.py
@@ -20,9 +20,9 @@
 
 def body(
     feat, w, bias, go, act_o, ig_o, wg_o, bg_o,
-    Xr, S, XV, XT, Wf, WT, Pt, RP, GOr, AC, Gr, GVp, WG, IG, IGb,
+    Xr, S, XV, XT, Wf, WT, Pt, RH, RP, GOr, AC, Gr, GVp, WG, IG, IGb,
     SC, RC, SX, RX, T2, SZ1, RZ1, T3, SZ2, RZ2, AA, bsum,
-    xs, xr, gos, gor, ws, wr, wl, ps, pr, gs, gr, acs, acr, igs, igr,
+    xs, xr, gos, gor, ws, wr, vs, vr, wl, hs, hr, ps, pr, gs, gr, acs, acr, igs, igr,
     cs, cr, x_s, x_r, z1s, z1r, z2s, z2r, y2s, y2r, y1s, y1r, yxs, yxr, ycs, ycr,
 ):
     dp = lax.axis_index("dp")
@@ -35,6 +35,9 @@
     za = lax.rem(z, 4)
     zb = z // 4
 
+    def flip_add(v, d):
+        return lax.rem(v + d, 4)
+
     def flip(v, d, n):
         out = v
         bit = 1
@@ -94,19 +97,29 @@
 
     lax.fori_loop(0, 5, lambda i, x: (feature_copies(i, True), x)[1], 0)
 
-    def weight_copies():
-        own = Wf.at[:, pl.ds(p * 128, 128), :]
-        first = remote(
-            w.at[pl.ds(0, 14)], Wf.at[pl.ds(0, 14), pl.ds(p * 128, 128), :], ws.at[0], wr.at[0], dev(pp=1 - p)
+    pieces = ((0, 9), (9, 10), (19, 8))
+
+    def weight_copy(j):
+        lo, n = pieces[j]
+        return remote(
+            w.at[pl.ds(lo, n), pl.ds(c * 64, 64)], Wf.at[pl.ds(lo, n), pl.ds(p * 128 + c * 64, 64)],
+            ws.at[j], wr.at[j], dev(uu=u if j == 2 else 1 - u, pp=1 - p),
         )
-        second = remote(
-            w.at[pl.ds(14, 13)], Wf.at[pl.ds(14, 13), pl.ds(p * 128, 128), :], ws.at[1], wr.at[1],
-            dev(uu=1 - u, pp=1 - p),
-        )
-        return first, second, pltpu.make_async_copy(w, own, wl.at[0])
-
-    for copy in weight_copies():
-        copy.start()
+
+    def weight_part(j, cc):
+        lo, n = pieces[j]
+        return Wf.at[pl.ds(lo, n), pl.ds((1 - p) * 128 + cc * 64, 64)]
+
+    def share_copy(j):
+        return remote(weight_part(j, c), weight_part(j, c), vs.at[j], vr.at[j], dev(cc=1 - c))
+
+    def share(j):
+        arrived(weight_part(j, c), wr.at[j])
+        share_copy(j).start()
+
+    for j in range(3):
+        weight_copy(j).start()
+    pltpu.make_async_copy(w, Wf.at[:, pl.ds(p * 128, 128), :], wl.at[0]).start()
 
     def grad_copies(i, start):
         row = 5 * s + i
@@ -156,22 +169,47 @@
             XV[v, n] = S[n, LEFT + d : LEFT + d + PITCH, 0:256].astype(BF)
         return x
 
+    share(0)
     lax.fori_loop(0, ROWS, spread, 0)
+    share(1)
+    for j in range(8):
+        lo, hi = 128 * j, min(960, 128 * j + 128)
+        piece = XV[0].reshape(ROWS * PITCH, 256)[lo:hi].astype(F32)
+        if hi - lo < 128:
+            piece = jnp.concatenate([piece, jnp.zeros((128 - (hi - lo), 256), F32)], axis=0)
+        XT[:, lo : lo + 128] = jnp.transpose(piece).astype(BF)
+    share(2)
     arrived(w, wl.at[0])
-    arrived(Wf.at[pl.ds(0, 14), pl.ds((1 - p) * 128, 128), :], wr.at[0])
-    arrived(Wf.at[pl.ds(14, 13), pl.ds((1 - p) * 128, 128), :], wr.at[1])
-
-    def partial_copy(k, d):
-        qq = flip(q, d, 4)
+
+    after, before, facing = flip_add(q, 1), flip_add(q, 3), flip_add(q, 2)
+    halves = ((0, 3), (3, 2))
+
+    def half_copy(k, e):
+        lo, n = halves[e]
         return remote(
-            Pt.at[k, pl.ds(5 * qq, 5)], RP.at[k, d - 1], ps.at[k, d - 1], pr.at[k, d - 1], dev(qq=qq)
+            Pt.at[k, pl.ds(5 * facing + lo, n)], RH.at[k, pl.ds(lo, n)], hs.at[k, e], hr.at[k, e],
+            dev(qq=before if e else after),
         )
+
+    def partial_copy(k, e):
+        qq = before if e else after
+        return remote(Pt.at[k, pl.ds(5 * qq, 5)], RP.at[k, e], ps.at[k, e], pr.at[k, e], dev(qq=qq))
+
+    def pass_on(k):
+        for e in range(2):
+            lo, n = halves[e]
+            arrived(RH.at[k, pl.ds(lo, n)], hr.at[k, e])
+            first = 5 * (before if e else after) + lo
+            for i in range(n):
+                Pt[k, first + i] += RH[k, lo + i]
+            partial_copy(k, e).start()
 
     def gather_copy(k, d):
         rows = Gr.at[k, pl.ds(5 * q, 5)]
         return remote(rows, rows, gs.at[k, d - 1], gr.at[k, d - 1], dev(qq=flip(q, d, 4)))
 
     for k in range(3):
+        arrived(weight_part(k, 1 - c), vr.at[k])
         for a in (0, -1, 1):
             sh = 6 * (k + 1) * a
             n0, n1 = max(0, -sh), ROWS - max(0, sh)
@@ -181,36 +219,26 @@
             ).reshape(rows * PITCH, 768)
             t = 9 * k + 3 * (a + 1)
             right = Wf[t : t + 3].reshape(768, 128)
-            part = jnp.dot(left, right, preferred_element_type=F32).reshape(rows, PITCH, 128)[:, :40]
+            part = jnp.dot(left, right, preferred_element_type=F32).reshape(rows, PITCH, 128)[:, :COLS]
             if a == 0:
                 Pt[k] = part
             else:
                 Pt[k, n0:n1] += part
-        for d in range(1, 4):
-            partial_copy(k, d).start()
-
-    for j in range(8):
-        lo, hi = 128 * j, min(960, 128 * j + 128)
-        piece = XV[0].reshape(ROWS * PITCH, 256)[lo:hi].astype(F32)
-        if hi - lo < 128:
-            piece = jnp.concatenate([piece, jnp.zeros((128 - (hi - lo), 256), F32)], axis=0)
-        XT[:, lo : lo + 128] = jnp.transpose(piece).astype(BF)
-
-    def turn(t, x):
-        WT[t] = jnp.transpose(Wf[t].astype(F32)).astype(BF)
-        return x
-
-    lax.fori_loop(0, 27, turn, 0)
+        for e in range(2):
+            half_copy(k, e).start()
+        if k > 0:
+            pass_on(k - 1)
+    pass_on(2)
+
     for i in range(5):
         arrived(GOr.at[i], gor.at[i])
 
     for k in range(3):
-        for d in range(1, 4):
-            arrived(RP.at[k, d - 1], pr.at[k, d - 1])
+        for e in range(2):
+            arrived(RP.at[k, e], pr.at[k, e])
         lanes = slice(128 * k, 128 * (k + 1))
         for i in range(5):
-            pre = Pt[k, 5 * q + i] + RP[k, 0, i] + RP[k, 1, i] + RP[k, 2, i] + bias[k : k + 1, :]
-            pre = pre[:COLS]
+            pre = Pt[k, 5 * q + i] + RP[k, 0, i] + RP[k, 1, i] + bias[k : k + 1, :]
             squash = jax.nn.sigmoid(pre)
             AC[i, :, lanes] = (pre * squash).astype(BF)
             slope = squash * (1.0 + pre * (1.0 - squash))
@@ -312,6 +340,12 @@
             cross_stage(k - 1)
     cross_stage(2)
 
+    def turn(t, x):
+        WT[t] = jnp.transpose(Wf[t].astype(F32)).astype(BF)
+        return x
+
+    lax.fori_loop(0, 27, turn, 0)
+
     for k in range(3):
         for a in (0, -1, 1):
             sh = 6 * (k + 1) * a
@@ -450,12 +484,14 @@
     lax.fori_loop(0, 5, lambda i, x: (grad_copies(i, False), x)[1], 0)
     lax.fori_loop(0, 5, lambda i, x: (act_copies(i, False), x)[1], 0)
     lax.fori_loop(0, ROWS, lambda n, x: (input_copies(n, False), x)[1], 0)
-    first, second, _ = weight_copies()
-    first.wait_send()
-    second.wait_send()
+    for j in range(3):
+        weight_copy(j).wait_send()
+        share_copy(j).wait_send()
     for k in range(3):
+        for e in range(2):
+            half_copy(k, e).wait_send()
+            partial_copy(k, e).wait_send()
         for d in range(1, 4):
-            partial_copy(k, d).wait_send()
             gather_copy(k, d).wait_send()
             cross_copy(k, d).wait_send()
         core_copy(k).wait_send()
@@ -490,15 +526,16 @@
     vmem = pl.BlockSpec(memory_space=pltpu.VMEM)
     scratch = [
         V((ROWS, COLS, 256), BF), V((ROWS, 128, 384), F32), V((7, ROWS, PITCH, 256), BF), V((256, 1024), BF),
-        V((27, 256, 128), BF), V((27, 128, 256), BF), V((3, ROWS, 40, 128), F32), V((3, 3, 5, 40, 128), F32),
+        V((27, 256, 128), BF), V((27, 128, 256), BF), V((3, ROWS, COLS, 128), F32), V((3, 5, COLS, 128), F32),
+        V((3, 2, 5, COLS, 128), F32),
         V((5, COLS, 384), BF), V((5, COLS, 384), BF), V((3, ROWS, COLS, 128), BF),
         V((3, ROWS + 2 * PAD, PITCH, 384), BF), V((TAPS, 2, 128, 128), F32), V((ROWS, PITCH, 256), F32),
         V((ROWS, COLS, 256), BF),
         V((TAPS, 2, 64, 128), BF), V((TAPS, 2, 64, 128), BF), V((2, 2, TAPS, 32, 128), BF), V((3, TAPS, 32, 128), BF),
         V((TAPS, 32, 128), F32), V((4, 7, 32, 128), BF), V((3, 7, 32, 128), BF), V((7, 32, 128), F32),
         V((7, 32, 128), BF), V((8, 32, 128), BF), V((2, 2, 4, 7, 32, 128), BF), V((8, 128), F32),
-        dma((5, 4, 2)), dma((ROWS, 2)), dma((5,)), dma((5,)), dma((2,)), dma((2,)), dma((1,)),
-        dma((3, 3)), dma((3, 3)), dma((3, 3)), dma((3, 3)), dma((5,)), dma((5,)), dma((ROWS, 2)), dma((5, 4, 2)),
+        dma((5, 4, 2)), dma((ROWS, 2)), dma((5,)), dma((5,)), dma((3,)), dma((3,)), dma((3,)), dma((3,)), dma((1,)),
+        dma((3, 2)), dma((3, 2)), dma((3, 2)), dma((3, 2)), dma((3, 3)), dma((3, 3)), dma((5,)), dma((5,)), dma((ROWS, 2)), dma((5, 4, 2)),
         dma((3,)), dma((3,)), dma((3, 3)), dma((3, 3)), dma((3,)), dma((3,)), dma((7,)), dma((8,)),
         dma((8,)), dma((8,)), dma((3,)), dma((3,)), dma((1,)), dma((1,)), dma((1,)), dma((1,)),
     ]

time: 145 us -> 136 us (0.938)
  the two profiles are of different devices: /device:TPU:1 before, /device:TPU:17 now
where the time goes in v2:
time: 136 us
  Pallas kernels  128 us (94%)
  local copies, waits for them, and re-layouts  6.82 us (5%)
    pallas_call x1, Pallas kernels, per_device(): pl.pallas_call(body, out_shape=(jax.ShapeDtypeStruct((1, 5, COLS, 384), B...  128 us
    unnamed x6, local copies, waits for them, and re-layouts  6.82 us

profile of v2, /device:TPU:17, one launch (start us, length us, event | category | flops | bytes accessed | tf_op | source)
XLA Modules:
  0.0 135.8 jit_solution(1222407581300660907)
XLA Ops:
  0.6 128.3 %pyramid.1 = (bf16[1,5,37,384]{3,2,1,0:T(8,128)(2,1)}, bf16[1,5,37,1024]{3,2,1,0:T(8,128)(2,1)}, f32[27,128,128]{2,1,0:T(8,128)}, f32[3,128]{1,0:T(4,128)}) custom-call(bf16[1,5,37,1024]{3,2,1,0:T(8,128)(2,1)} %feat.1, bf16[27,128,128]{2,1,0:T(8,128)(2,1)} %bitcast.3, f32[3,128]{1,0:T(4,128)} %bias.1, bf16[1,5,37,384]{3,2,1,0:T(8,128)(2,1)} %go.1), custom_call_target="tpu_custom_call" | custom-call | tf_op jit(solution)/shard_map/pyramid/pallas_call | solution.py:542
  128.9 1.6 %copy.12 = bf16[1,5,37,384]{3,2,1,0:T(8,128)(2,1)} copy(bf16[1,5,37,384]{3,2,1,0:T(8,128)(2,1)} %get-tuple-element.16) | data formatting | bytes 284160
  130.5 1.8 %copy.13 = bf16[1,5,37,1024]{3,2,1,0:T(8,128)(2,1)} copy(bf16[1,5,37,1024]{3,2,1,0:T(8,128)(2,1)} %get-tuple-element.17) | data formatting | bytes 757760
  132.3 0.0 copy-start
  132.3 2.9 %copy.14 = f32[3,9,128,128]{3,2,1,0:T(8,128)} copy(f32[3,9,128,128]{3,2,1,0:T(8,128)} %bitcast.2) | data formatting | bytes 3538944
  135.2 0.0 copy-done
  135.2 0.6 copy.15
Async XLA Ops:
  132.3 2.9 %copy-start = (f32[3,128]{1,0:T(4,128)S(1)}, f32[3,128]{1,0:T(4,128)}, u32[]{:S(2)}) copy-start(f32[3,128]{1,0:T(4,128)} %get-tuple-element.19) | copy-start | bytes 4612
